TPU v7x, 128 devices: a whole 4x4x4 slice. The times are simulated.
128 devices in a mesh: replica: 32 (over y, x, z_hi), tensor: 4 (over z_lo, core).
Axes of the slice: x: 4, y: 4, z: 4 (z_hi: 2, z_lo: 2; z = z_hi * 2 + z_lo), core: 2. Of those that a mesh axis runs over, the one named last changes fastest.
Arguments:
- weights: bfloat16 [32, 7168, 2048], P('replica', 'tensor'), may hold values from -6 to 6
- hidden: bfloat16 [32, 2, 512, 7168], P('replica', None, None, 'tensor'), may hold values from -6 to 6
- targets: bfloat16 [32, 2, 512, 2048], P('replica'), may hold values from -6 to 6
- norm_gain: float32 [2048], replicated, may hold values from 0.5 to 2
- stragglers: int32 [2, 32], replicated, may hold values 0 or 1
Outputs:
- new_weights: bfloat16 [32, 7168, 2048], P('replica', 'tensor')
All inputs are finite; a program needn't handle non-finite values.
Results may differ from a plain program's by a relative error of at most 0.011.
Values may be sent and summed in bfloat16 or wider, within the bound.
No kernel may reach another device: no remote copies, remote signals or barrier semaphores. Data moves between devices by JAX's collectives and lax.ppermute only.
A program may use at most 128 MiB of HBM per device.

v0:
```python
import jax
import jax.numpy as jnp
from jax import lax
from jax.sharding import PartitionSpec as P

FF = 7168
STEPS = 2
eps = 1e-05
learn_rate = 0.5


def partner(block, axis, apart):
    count = lax.axis_size(axis)
    route = []
    for low in range(count):
        high = low | 1 << apart
        if high != low and high < count:
            route += [(low, high), (high, low)]
    return lax.ppermute(block, axis, route)


def contract_rows(left, right):
    return lax.dot_general(
        left, right, (((0,), (0,)), ((), ())), preferred_element_type=jnp.float32
    )


def norm_backward(outputs, target_rows, norm_gain):
    squares = jnp.mean(outputs * outputs, axis=-1, keepdims=True)
    inverse = lax.rsqrt(squares + eps)
    normed = outputs * inverse
    weighted = (normed * norm_gain - target_rows.astype(jnp.float32)) * norm_gain
    cross_mean = jnp.mean(weighted * normed, axis=-1, keepdims=True)
    return (inverse * (weighted - normed * cross_mean)).astype(jnp.bfloat16)


def on_device(weights, hidden, targets, norm_gain, stragglers):
    replica_index = lax.axis_index("replica")
    levels = lax.axis_size("replica").bit_length() - 1
    factor = FF ** (-0.5)
    weight_block = weights[0]
    for update_step in range(STEPS):
        bit_index = update_step % levels
        hidden_rows = hidden[0, update_step]
        target_rows = targets[0, update_step]
        terms = factor * jnp.dot(hidden_rows, weight_block, preferred_element_type=jnp.float32)
        outputs = lax.psum(terms.astype(jnp.bfloat16), "tensor").astype(jnp.float32)
        grad_out = norm_backward(outputs, target_rows, norm_gain)
        grad_weight = (factor * contract_rows(hidden_rows, grad_out)).astype(jnp.bfloat16)
        updated = (
            weight_block.astype(jnp.float32) - learn_rate * grad_weight.astype(jnp.float32)
        ).astype(jnp.bfloat16)
        paired = partner(updated, "replica", bit_index)
        partner_index = jnp.bitwise_xor(replica_index, jnp.int32(1 << bit_index))
        mask_row = stragglers[update_step]
        self_late = lax.dynamic_index_in_dim(mask_row, replica_index, keepdims=False)
        partner_late = lax.dynamic_index_in_dim(mask_row, partner_index, keepdims=False)
        keep_pair = (self_late == 0) & (partner_late == 0)
        averaged = ((updated.astype(jnp.float32) + paired.astype(jnp.float32)) * 0.5).astype(
            jnp.bfloat16
        )
        weight_block = jnp.where(keep_pair, averaged, updated)
    return weight_block[None]


def solution(mesh):
    placed = (
        P("replica", "tensor", None),
        P("replica", None, None, "tensor"),
        P("replica", None, None, None),
        P(),
        P(),
    )
    return jax.shard_map(
        on_device,
        mesh=mesh,
        in_specs=placed,
        out_specs=P("replica", "tensor", None),
        check_vma=False,
    )
```

profile of v0, /device:TPU:1, one launch (start us, length us, event | category | flops | bytes accessed | tf_op | source)
XLA Modules:
  0.0 542.5 jit_solution(9329195445584160518)
XLA Ops:
  6.5 0.0 all-reduce.3.cloned.1.call-start
  6.5 8.9 %multiply_convert_fusion.5 = bf16[512,2048]{1,0:T(8,128)(2,1)} fusion(bf16[1,1792,2048]{2,1,0:T(8,128)(2,1)} %param.5, bf16[1,2,512,1792]{3,2,1,0:T(8,128)(2,1)} %param.6), kind=kOutput, calls=%fused_computation.38 | convolution fusion | flops 3760193536 | bytes 11272192 | tf_op jit(solution)/shard_map/dot_general | solution.py:46
  15.5 0.0 all-reduce.3.cloned.1.call-update
  15.5 0.0 copy-start.6
  15.5 0.0 all-reduce.5.cloned.1.call-start
  15.6 9.9 %copy.6 = bf16[1,1792,2048]{1,2,0:T(8,128)(2,1)} copy(bf16[1,1792,2048]{2,1,0:T(8,128)(2,1)} %param.5) | data formatting | bytes 14680064 | tf_op args[0]
  25.5 51.2 %all-reduce.3.cloned.1.call-done = bf16[512,2048]{1,0:T(8,128)(2,1)} async-done(((bf16[512,2048]{1,0:T(8,128)(2,1)}), bf16[512,2048]{1,0:T(8,128)(2,1)}) %all-reduce.3.cloned.1.call-update) | async-done | bytes 2097168 | tf_op jit(solution)/shard_map/psum | solution.py:47
  76.7 0.0 copy-start
  76.7 0.0 copy-start.4
  76.7 2.2 fusion.19
  79.0 0.0 copy-done.6
  79.0 3.7 fusion.15
  82.7 0.0 copy-done
  82.7 0.0 copy-done.4
  82.7 0.0 copy-start.7
  82.7 9.9 %fusion.1 = bf16[1792,2048]{0,1:T(8,128)(2,1)} fusion(bf16[1,1792,2048]{1,2,0:T(8,128)(2,1)} %copy.6, bf16[512,2048]{1,0:T(8,128)(2,1)S(1)} %copy-done, f32[512]{0:T(512)S(1)} %broadcast_multiply_fusion.1, f32[2048]{0:T(1024)S(1)} %copy-done.6, f32[512]{0:T(512)S(1)} %add_rsqrt_fusion.1, bf16[1,2,512,2048]{3,2,1,0:T(8,128)(2,1)S(1)} %copy-done.4, ...), kind=kOutput, calls=%fused_computation.3 | convolution fusion | flops 3794272256 | bytes 20721664 | tf_op jit(solution)/shard_map/dot_general | solution.py:23
  92.6 2.6 collective-permute-start
  95.2 0.0 copy-done.7
  95.2 0.7 constant_dynamic-slice_fusion
  97.1 156.6 %collective-permute-done = bf16[1792,2048]{0,1:T(8,128)(2,1)} collective-permute-done((bf16[1792,2048]{0,1:T(8,128)(2,1)}, bf16[1792,2048]{0,1:T(8,128)(2,1)}, u32[]{:S(2)}, u32[]{:S(2)}) %collective-permute-start) | collective-permute-done | bytes 7340064 | tf_op jit(solution)/shard_map/ppermute | solution.py:19
  253.7 13.1 %fusion.29 = bf16[512,2048]{1,0:T(8,128)(2,1)} fusion(bf16[1,2,512,1792]{3,2,1,0:T(8,128)(2,1)} %param.6, bf16[1792,2048]{0,1:T(8,128)(2,1)} %fusion.1, bf16[1792,2048]{0,1:T(8,128)(2,1)} %collective-permute-done, pred[]{:T(512)} %bitcast.1), kind=kOutput, calls=%fused_computation.39 | convolution fusion | flops 3782213632 | bytes 18612736 | tf_op jit(solution)/shard_map/dot_general | solution.py:46
  266.8 0.0 all-reduce.5.cloned.1.call-update
  266.8 59.5 %all-reduce.5.cloned.1.call-done = bf16[512,2048]{1,0:T(8,128)(2,1)} async-done(((bf16[512,2048]{1,0:T(8,128)(2,1)}), bf16[512,2048]{1,0:T(8,128)(2,1)}) %all-reduce.5.cloned.1.call-update) | async-done | bytes 2097168 | tf_op jit(solution)/shard_map/psum | solution.py:47
  326.3 0.0 copy-start.1
  326.3 0.0 copy-start.5
  326.3 2.2 fusion.26
  328.6 3.7 fusion.22
  332.3 0.0 copy-done.1
  332.3 0.0 copy-done.5
  332.3 14.4 %fusion = bf16[1792,2048]{0,1:T(8,128)(2,1)S(1)} fusion(bf16[512,2048]{1,0:T(8,128)(2,1)S(1)} %copy-done.1, f32[512]{0:T(512)S(1)} %broadcast_multiply_fusion, f32[512]{0:T(512)S(1)} %add_rsqrt_fusion, f32[2048]{0:T(1024)S(1)} %copy-done.6, bf16[1,2,512,2048]{3,2,1,0:T(8,128)(2,1)S(1)} %copy-done.5, bf16[1,2,512,1792]{3,2,1,0:T(8,128)(2,1)} %param.6, ...), kind=kOutput, calls=%fused_computation.1 | convolution fusion | flops 3816292352 | bytes 28062208 | tf_op jit(solution)/shard_map/dot_general | solution.py:23
  346.7 0.0 copy-start.2
  346.7 3.0 copy-done.2
  349.7 1.2 collective-permute-start.1
  352.2 156.7 %collective-permute-done.1 = bf16[1792,2048]{0,1:T(8,128)(2,1)S(1)} collective-permute-done((bf16[1792,2048]{0,1:T(8,128)(2,1)S(1)}, bf16[1792,2048]{0,1:T(8,128)(2,1)S(1)}, u32[]{:S(2)}, u32[]{:S(2)}) %collective-permute-start.1) | collective-permute-done | bytes 7340064 | tf_op jit(solution)/shard_map/ppermute | solution.py:19
  509.0 0.0 copy-start.3
  509.0 3.0 copy-done.3
  511.9 13.3 %fusion.4 = bf16[1,1792,2048]{1,2,0:T(8,128)(2,1)} fusion(bf16[1792,2048]{0,1:T(8,128)(2,1)} %copy-done.2, bf16[1792,2048]{0,1:T(8,128)(2,1)} %copy-done.3, pred[]{:T(512)} %bitcast), kind=kLoop, calls=%fused_computation.10 | loop fusion | flops 22020096 | bytes 22020096 | tf_op jit(solution)/shard_map/broadcast_in_dim | solution.py:63
  525.3 10.4 %copy.8 = bf16[1,1792,2048]{2,1,0:T(8,128)(2,1)} copy(bf16[1,1792,2048]{1,2,0:T(8,128)(2,1)} %fusion.4) | data formatting | bytes 14680064 | tf_op jit(solution)/shard_map/broadcast_in_dim | solution.py:63
  (5 shorter events, 0.0 us)
Async XLA Ops:
  6.5 70.2 %all-reduce.3.cloned.1.call-start = ((), (), s32[]{:S(2)}) async-start(), calls=%async_computation | async-start | bytes 4194304 | tf_op jit(solution)/shard_map/psum | solution.py:47
  15.5 63.5 %copy-start.6 = (f32[2048]{0:T(1024)S(1)}, f32[2048]{0:T(1024)}, u32[]{:S(2)}) copy-start(f32[2048]{0:T(1024)} %param.8) | copy-start | bytes 24580
  15.5 310.8 %all-reduce.5.cloned.1.call-start = ((), (), s32[]{:S(2)}) async-start(), calls=%async_computation.1 | async-start | bytes 4194304 | tf_op jit(solution)/shard_map/psum | solution.py:47
  76.7 5.9 %copy-start = (bf16[512,2048]{1,0:T(8,128)(2,1)S(1)}, bf16[512,2048]{1,0:T(8,128)(2,1)}, u32[]{:S(2)}) copy-start(bf16[512,2048]{1,0:T(8,128)(2,1)} %all-reduce.3.cloned.1.call-done) | copy-start | bytes 6291460
  76.7 5.9 %copy-start.4 = (bf16[1,2,512,2048]{3,2,1,0:T(8,128)(2,1)S(1)}, bf16[1,2,512,2048]{3,2,1,0:T(8,128)(2,1)}, u32[]{:S(2)}) copy-start(bf16[1,2,512,2048]{3,2,1,0:T(8,128)(2,1)} %param.7) | copy-start | bytes 12582916
  82.7 12.5 %copy-start.7 = (s32[2,32]{1,0:T(2,128)S(1)}, s32[2,32]{1,0:T(2,128)}, u32[]{:S(2)}) copy-start(s32[2,32]{1,0:T(2,128)} %param.9) | copy-start | bytes 772
  92.6 161.1 %collective-permute-start = (bf16[1792,2048]{0,1:T(8,128)(2,1)}, bf16[1792,2048]{0,1:T(8,128)(2,1)}, u32[]{:S(2)}, u32[]{:S(2)}) collective-permute-start(bf16[1792,2048]{0,1:T(8,128)(2,1)} %fusion.1), channel_id=1, source_target_pairs={{0,4},{4,0},{8,12},{12,8},{16,20},{20,16},{24,28},{28,24},{32,36},... | collective-permute-start | bytes 22020104 | tf_op jit(solution)/shard_map/ppermute | solution.py:19
  326.3 5.9 %copy-start.1 = (bf16[512,2048]{1,0:T(8,128)(2,1)S(1)}, bf16[512,2048]{1,0:T(8,128)(2,1)}, u32[]{:S(2)}) copy-start(bf16[512,2048]{1,0:T(8,128)(2,1)} %all-reduce.5.cloned.1.call-done) | copy-start | bytes 6291460
  326.3 5.9 %copy-start.5 = (bf16[1,2,512,2048]{3,2,1,0:T(8,128)(2,1)S(1)}, bf16[1,2,512,2048]{3,2,1,0:T(8,128)(2,1)}, u32[]{:S(2)}) copy-start(bf16[1,2,512,2048]{3,2,1,0:T(8,128)(2,1)} %param.7) | copy-start | bytes 12582916
  346.7 3.1 copy-start.2
  349.7 159.2 %collective-permute-start.1 = (bf16[1792,2048]{0,1:T(8,128)(2,1)S(1)}, bf16[1792,2048]{0,1:T(8,128)(2,1)S(1)}, u32[]{:S(2)}, u32[]{:S(2)}) collective-permute-start(bf16[1792,2048]{0,1:T(8,128)(2,1)S(1)} %fusion), channel_id=1, source_target_pairs={{0,8},{8,0},{4,12},{12,4},{16,24},{24,16},{20,28},{28,20},{32,40},... | collective-permute-start | bytes 22020104 | tf_op jit(solution)/shard_map/ppermute | solution.py:19
  509.0 3.0 copy-start.3
Sparse Core Ops, SparseCore 0:
  15.6 61.0 all-reduce.2
  267.0 59.3 all-reduce.4
where the time goes:
time: 543 us
  waiting for transfers between devices  424 us (78%)
  matrix products  46.4 us (9%)
  local copies, waits for them, and re-layouts  27.1 us (5%)
  other arithmetic  25.2 us (5%)
  between operations  16 us (3%)
    ppermute x2, waiting for transfers between devices, partner(): return lax.ppermute(block, axis, route)  313 us
    psum x2, waiting for transfers between devices, on_device(): outputs = lax.psum(terms.astype(jnp.bfloat16), 'tensor').astype(jnp.float32)  111 us
    dot_general x2, matrix products, contract_rows(): lax.dot_general(left, right, (((0,), (0,)), ((), ())), preferred_element_...  24.3 us
    dot_general x2, matrix products, on_device(): jnp.dot(hidden_rows, weight_block, preferred_element_type=jnp.float32)  22.1 us
    unnamed x17, local copies, waits for them, and re-layouts  16 us
    broadcast_in_dim x1, other arithmetic, on_device(): return weight_block[None]  13.3 us
  transfers between devices with their start and end apart: 4, of which 4 were waited for; matrix products, arithmetic and copies ran while one was open for 2% of the time, Pallas kernels for 0%

commit v1 on v0

--- a/solution.py
+++ b/solution.py
@@ -44,7 +44,9 @@
         hidden_rows = hidden[0, update_step]
         target_rows = targets[0, update_step]
         terms = factor * jnp.dot(hidden_rows, weight_block, preferred_element_type=jnp.float32)
-        outputs = lax.psum(terms.astype(jnp.bfloat16), "tensor").astype(jnp.float32)
+        outputs = jnp.sum(lax.all_gather(terms.astype(jnp.bfloat16), "tensor"), axis=0).astype(
+            jnp.float32
+        )
         grad_out = norm_backward(outputs, target_rows, norm_gain)
         grad_weight = (factor * contract_rows(hidden_rows, grad_out)).astype(jnp.bfloat16)
         updated = (

time: 543 us -> 625 us (1.15)
  waiting for transfers between devices: 424 us -> 471 us
  local copies, waits for them, and re-layouts: 27.1 us -> 44.6 us
  other arithmetic: 25.2 us -> 41.3 us
    all_gather x0 -> x2, waiting for transfers between devices: none -> 158 us  [on_device(): lax.all_gather(terms.astype(jnp.bfloat16), 'tensor')]
    psum x2 -> x0, waiting for transfers between devices: 111 us -> none  [on_device(): outputs = lax.psum(terms.astype(jnp.bfloat16), 'tensor').astype(jnp.float32)]
    reduce_sum x0 -> x2, other arithmetic: none -> 20.7 us  [on_device(): jnp.sum(lax.all_gather(terms.astype(jnp.bfloat16), 'tensor'), axis=0)]
    all_gather x0 -> x1, local copies, waits for them, and re-layouts: none -> 14.6 us  [on_device(): lax.all_gather(terms.astype(jnp.bfloat16), 'tensor')]
    unnamed x17 -> x13, local copies, waits for them, and re-layouts: 16 us -> 16 us
where the time goes in v1:
time: 625 us; the launch traced here: 624 us
  waiting for transfers between devices  471 us (75%)
  matrix products  46.8 us (7%)
  local copies, waits for them, and re-layouts  44.6 us (7%)
  other arithmetic  41.3 us (7%)
  between operations  16 us (3%)
    ppermute x2, waiting for transfers between devices, partner(): return lax.ppermute(block, axis, route)  313 us
    all_gather x2, waiting for transfers between devices, on_device(): lax.all_gather(terms.astype(jnp.bfloat16), 'tensor')  158 us
    dot_general x2, matrix products, contract_rows(): lax.dot_general(left, right, (((0,), (0,)), ((), ())), preferred_element_...  24.3 us
    dot_general x2, matrix products, on_device(): jnp.dot(hidden_rows, weight_block, preferred_element_type=jnp.float32)  22.5 us
    reduce_sum x2, other arithmetic, on_device(): jnp.sum(lax.all_gather(terms.astype(jnp.bfloat16), 'tensor'), axis=0)  20.7 us
    unnamed x13, local copies, waits for them, and re-layouts  16 us
    all_gather x1, local copies, waits for them, and re-layouts, on_device(): lax.all_gather(terms.astype(jnp.bfloat16), 'tensor')  14.6 us
    broadcast_in_dim x1, other arithmetic, on_device(): return weight_block[None]  13.5 us
  transfers between devices with their start and end apart: 4, of which 4 were waited for; matrix products, arithmetic and copies ran while one was open for 2% of the time, Pallas kernels for 0%

profile of v1, /device:TPU:1, one launch (start us, length us, event | category | flops | bytes accessed | tf_op | source)
XLA Modules:
  0.0 623.6 jit_solution(6766217984965176032)
XLA Ops:
  6.5 0.0 all-gather.5.cloned.1.call-start
  6.5 9.0 %multiply_convert_fusion.5 = bf16[512,2048]{1,0:T(8,128)(2,1)} fusion(bf16[1,1792,2048]{2,1,0:T(8,128)(2,1)} %param.5, bf16[1,2,512,1792]{3,2,1,0:T(8,128)(2,1)} %param.6), kind=kOutput, calls=%fused_computation.50 | convolution fusion | flops 3760193536 | bytes 11272192 | tf_op jit(solution)/shard_map/dot_general | solution.py:46
  15.5 0.0 all-gather.5.cloned.1.call-update
  15.6 0.0 all-gather.7.cloned.1.call-start
  15.6 9.9 %copy.12 = bf16[1,1792,2048]{1,2,0:T(8,128)(2,1)} copy(bf16[1,1792,2048]{2,1,0:T(8,128)(2,1)} %param.5) | data formatting | bytes 14680064 | tf_op args[0]
  25.6 75.3 %all-gather.5.cloned.1.call-done = bf16[2048,2048]{1,0:T(8,128)(2,1)} async-done(((bf16[512,2048]{1,0:T(8,128)(2,1)}), bf16[2048,2048]{1,0:T(8,128)(2,1)}) %all-gather.5.cloned.1.call-update) | async-done | bytes 8388624 | tf_op jit(solution)/shard_map/all_gather | solution.py:47
  100.8 0.0 copy-start.4
  100.8 5.7 reduce_sum.60
  106.5 0.0 copy-start.2
  106.5 0.5 fusion.25
  107.0 0.0 copy-done.4
  107.0 3.1 fusion.16
  110.1 0.0 copy-done.2
  110.1 0.0 copy-start.5
  110.1 9.9 %fusion.1 = bf16[1792,2048]{0,1:T(8,128)(2,1)} fusion(bf16[1,1792,2048]{1,2,0:T(8,128)(2,1)} %copy.12, bf16[512,2048]{1,0:T(8,128)(2,1)S(1)} %reduce_sum.60, f32[512]{0:T(512)S(1)} %broadcast_multiply_fusion.1, f32[2048]{0:T(1024)S(1)} %copy-done.4, f32[512]{0:T(512)S(1)} %add_rsqrt_fusion.1, bf16[1,2,512,2048]{3,2,1,0:T(8,128)(2,1)S(1)} %copy-done.2, ...), kind=kOutput, calls=%fused_computation.3 | convolution fusion | flops 3794272256 | bytes 20721664 | tf_op jit(solution)/shard_map/dot_general | solution.py:23
  120.0 2.6 collective-permute-start
  122.6 0.0 copy-done.5
  122.6 0.7 constant_dynamic-slice_fusion
  124.5 156.5 %collective-permute-done = bf16[1792,2048]{0,1:T(8,128)(2,1)} collective-permute-done((bf16[1792,2048]{0,1:T(8,128)(2,1)}, bf16[1792,2048]{0,1:T(8,128)(2,1)}, u32[]{:S(2)}, u32[]{:S(2)}) %collective-permute-start) | collective-permute-done | bytes 7340064 | tf_op jit(solution)/shard_map/ppermute | solution.py:19
  281.0 13.5 %fusion.35 = bf16[512,2048]{0,1:T(8,128)(2,1)} fusion(bf16[1,2,512,1792]{3,2,1,0:T(8,128)(2,1)} %param.6, bf16[1792,2048]{0,1:T(8,128)(2,1)} %fusion.1, bf16[1792,2048]{0,1:T(8,128)(2,1)} %collective-permute-done, pred[]{:T(512)} %bitcast.1), kind=kOutput, calls=%fused_computation.51 | convolution fusion | flops 3782213632 | bytes 18612736 | tf_op jit(solution)/shard_map/dot_general | solution.py:46
  294.5 0.0 all-gather.7.cloned.1.call-update
  294.6 82.6 %all-gather.7.cloned.1.call-done = bf16[2048,2048]{0,1:T(8,128)(2,1)} async-done(((bf16[512,2048]{0,1:T(8,128)(2,1)}), bf16[2048,2048]{0,1:T(8,128)(2,1)}) %all-gather.7.cloned.1.call-update) | async-done | bytes 8388624 | tf_op jit(solution)/shard_map/all_gather | solution.py:47
  377.2 14.6 %reshape.261 = bf16[4,512,2048]{1,0,2:T(4,128)(2,1)} reshape(bf16[2048,2048]{0,1:T(8,128)(2,1)} %all-gather.7.cloned.1.call-done) | data formatting | bytes 16777216 | tf_op jit(solution)/shard_map/all_gather | solution.py:47
  391.7 15.0 %reduce_sum.63 = bf16[512,2048]{0,1:T(8,128)(2,1)} reduce(bf16[4,512,2048]{1,0,2:T(4,128)(2,1)} %reshape.261, bf16[]{:T(256)} %constant.45.clone.1), dimensions={0}, to_apply=%region_3.4 | reduce | flops 3145728 | bytes 10485762 | tf_op jit(solution)/shard_map/reduce_sum | solution.py:47
  406.7 2.9 copy.13
  409.6 0.0 copy-start.3
  409.6 0.5 fusion.29
  410.1 3.1 fusion.13
  413.2 0.0 copy-done.3
  413.2 14.4 %fusion = bf16[1792,2048]{0,1:T(8,128)(2,1)S(1)} fusion(bf16[512,2048]{1,0:T(8,128)(2,1)S(1)} %copy.13, f32[512]{0:T(512)S(1)} %broadcast_multiply_fusion, f32[512]{0:T(512)S(1)} %add_rsqrt_fusion, f32[2048]{0:T(1024)S(1)} %copy-done.4, bf16[1,2,512,2048]{3,2,1,0:T(8,128)(2,1)S(1)} %copy-done.3, bf16[1,2,512,1792]{3,2,1,0:T(8,128)(2,1)} %param.6, ...), kind=kOutput, calls=%fused_computation.1 | convolution fusion | flops 3816292352 | bytes 28062208 | tf_op jit(solution)/shard_map/dot_general | solution.py:23
  427.6 0.0 copy-start
  427.6 3.0 copy-done
  430.7 1.2 collective-permute-start.1
  433.1 156.7 %collective-permute-done.1 = bf16[1792,2048]{0,1:T(8,128)(2,1)S(1)} collective-permute-done((bf16[1792,2048]{0,1:T(8,128)(2,1)S(1)}, bf16[1792,2048]{0,1:T(8,128)(2,1)S(1)}, u32[]{:S(2)}, u32[]{:S(2)}) %collective-permute-start.1) | collective-permute-done | bytes 7340064 | tf_op jit(solution)/shard_map/ppermute | solution.py:19
  589.9 0.0 copy-start.1
  589.9 3.0 copy-done.1
  592.8 13.5 %fusion.4 = bf16[1,1792,2048]{1,2,0:T(8,128)(2,1)} fusion(bf16[1792,2048]{0,1:T(8,128)(2,1)} %copy-done, bf16[1792,2048]{0,1:T(8,128)(2,1)} %copy-done.1, pred[]{:T(512)} %bitcast), kind=kLoop, calls=%fused_computation.10 | loop fusion | flops 22020096 | bytes 22020096 | tf_op jit(solution)/shard_map/broadcast_in_dim | solution.py:65
  606.3 10.4 %copy.14 = bf16[1,1792,2048]{2,1,0:T(8,128)(2,1)} copy(bf16[1,1792,2048]{1,2,0:T(8,128)(2,1)} %fusion.4) | data formatting | bytes 14680064 | tf_op jit(solution)/shard_map/broadcast_in_dim | solution.py:65
  (5 shorter events, 0.0 us)
Async XLA Ops:
  6.5 94.3 %all-gather.5.cloned.1.call-start = ((), (), s32[]{:S(2)}) async-start(), calls=%async_computation | async-start | bytes 10485760 | tf_op jit(solution)/shard_map/all_gather | solution.py:47
  15.6 361.6 %all-gather.7.cloned.1.call-start = ((), (), s32[]{:S(2)}) async-start(), calls=%async_computation.1 | async-start | bytes 10485760 | tf_op jit(solution)/shard_map/all_gather | solution.py:47
  100.8 6.2 copy-start.4
  106.5 3.6 copy-start.2
  110.1 12.5 %copy-start.5 = (s32[2,32]{1,0:T(2,128)S(1)}, s32[2,32]{1,0:T(2,128)}, u32[]{:S(2)}) copy-start(s32[2,32]{1,0:T(2,128)} %param.9) | copy-start | bytes 772
  120.0 161.0 %collective-permute-start = (bf16[1792,2048]{0,1:T(8,128)(2,1)}, bf16[1792,2048]{0,1:T(8,128)(2,1)}, u32[]{:S(2)}, u32[]{:S(2)}) collective-permute-start(bf16[1792,2048]{0,1:T(8,128)(2,1)} %fusion.1), channel_id=1, source_target_pairs={{0,4},{4,0},{8,12},{12,8},{16,20},{20,16},{24,28},{28,24},{32,36},... | collective-permute-start | bytes 22020104 | tf_op jit(solution)/shard_map/ppermute | solution.py:19
  409.6 3.6 copy-start.3
  427.6 3.1 copy-start
  430.7 159.2 %collective-permute-start.1 = (bf16[1792,2048]{0,1:T(8,128)(2,1)S(1)}, bf16[1792,2048]{0,1:T(8,128)(2,1)S(1)}, u32[]{:S(2)}, u32[]{:S(2)}) collective-permute-start(bf16[1792,2048]{0,1:T(8,128)(2,1)S(1)} %fusion), channel_id=1, source_target_pairs={{0,8},{8,0},{4,12},{12,4},{16,24},{24,16},{20,28},{28,20},{32,40},... | collective-permute-start | bytes 22020104 | tf_op jit(solution)/shard_map/ppermute | solution.py:19
  589.9 3.0 copy-start.1
Sparse Core Ops, SparseCore 0:
  15.7 85.0 all-gather.4
  294.7 82.4 all-gather.6
